TPU v7x, 32 devices: a whole 2x2x4 slice. The times are simulated.
32 devices in a mesh: req: 8 (over y, x, core), mp: 4 (over z).
Axes of the slice: x: 2, y: 2, z: 4, core: 2. Of those that a mesh axis runs over, the one named last changes fastest.
Arguments:
- latents: bfloat16 [16, 1, 384, 416], P('req', None, 'mp'), may hold values from -12 to 12
- prior_frame_cache: bfloat16 [16, 2, 384, 416], P('req', None, 'mp'), may hold values from -6 to 6
- move_to: int32 [16], P('req'), may hold values from 0 to 15, as said below
- counts: int32 [8], P('req'), may hold values from 1 to 2, as said below
- norm_gain: bfloat16 [384], P('mp'), may hold values from 0.5 to 1.5
- conv_weight: bfloat16 [27, 384, 384], P(None, 'mp'), may hold values from -0.0625 to 0.0625
- conv_bias: float32 [384], P('mp'), may hold values from -1.5 to 1.5
Outputs:
- decoded: bfloat16 [16, 1, 384, 416], P('req', None, 'mp')
- new_cache: bfloat16 [16, 2, 384, 416], P('req', None, 'mp')
Inputs may be any that keep to these rules, and one draw needn't show every extreme that they name: move_to is a permutation of the slots; a stream's new slot lies on its old index of req or on the next or previous one, the last and first index being neighbours; every index hands exactly 1 stream to each neighbour and takes the same number back from it. `counts`: some index of req is full and some other holds a single stream.
All inputs are finite; a program needn't handle non-finite values.
Results may differ from a plain program's by a relative error of at most 0.0018.
Values may be sent and summed in bfloat16 or wider, within the bound.
A program may use at most 64 MiB of HBM per device.

v0:
```python
import jax
import jax.numpy as jnp
from jax import lax
from jax.sharding import PartitionSpec as P

SECTION_CHANNELS = 384
LATENT_COLUMNS = 104


def shifted_2(block, axis, distance):
    devices = range(lax.axis_size(axis))
    route = [((i - distance) % len(devices), i) for i in devices]
    return lax.ppermute(block, axis, route)


def apply_taps(running, shard_in, weights, row_width):
    frames = shard_in.shape[1] - 2
    pixels = shard_in.shape[3]
    padded = jnp.pad(shard_in, ((0, 0), (0, 0), (0, 0), (row_width + 1, row_width + 1)))
    column = jnp.arange(pixels + 2 * row_width) % row_width
    for step_x in range(3):
        inside = ((column + step_x - 1 >= 0) & (column + step_x - 1 < row_width)).astype(
            shard_in.dtype
        )
        shifted = padded[:, :, :, step_x : step_x + pixels + 2 * row_width] * inside
        for step_y in range(3):
            window = shifted[:, :, :, step_y * row_width : step_y * row_width + pixels]
            for step_t in range(3):
                running = running + jnp.einsum(
                    "oc,stcp->stop",
                    weights[step_t * 9 + step_y * 3 + step_x],
                    window[:, step_t : step_t + frames],
                    preferred_element_type=jnp.float32,
                )
    return running


def pack_slots(prior_frame_cache, chosen, target, capacity):
    ranking = jnp.cumsum(chosen.astype(jnp.int32)) - 1
    picker = (chosen[None, :] & (ranking[None, :] == jnp.arange(capacity)[:, None])).astype(
        jnp.bfloat16
    )
    blocks = jnp.einsum(
        "cs,sfkp->cfkp", picker, prior_frame_cache, preferred_element_type=jnp.float32
    ).astype(jnp.bfloat16)
    labels = (jnp.dot(picker.astype(jnp.float32), (target + 1).astype(jnp.float32)) - 1.0).astype(
        jnp.bfloat16
    )
    return (blocks, labels)


def migrate(prior_frame_cache, move_to):
    slot_count = prior_frame_cache.shape[0]
    member_slots = lax.axis_size("req")
    position = lax.axis_index("req")
    capacity = slot_count // 2
    device = move_to // slot_count
    target = move_to % slot_count
    offset = (device - position) % member_slots
    goes_right = offset == 1
    goes_left = offset == member_slots - 1
    stays_put = offset == 0
    blocks_right, labels_right = pack_slots(prior_frame_cache, goes_right, target, capacity)
    blocks_left, labels_left = pack_slots(prior_frame_cache, goes_left, target, capacity)
    from_left = shifted_2((blocks_right, labels_right), "req", 1)
    from_right = shifted_2((blocks_left, labels_left), "req", -1)
    sources = jnp.concatenate([prior_frame_cache, from_left[0], from_right[0]], axis=0)
    own_labels = jnp.where(stays_put, target, -1).astype(jnp.float32)
    labels = jnp.concatenate(
        [own_labels, from_left[1].astype(jnp.float32), from_right[1].astype(jnp.float32)]
    )
    placing = (labels[None, :] == jnp.arange(slot_count, dtype=jnp.float32)[:, None]).astype(
        jnp.bfloat16
    )
    return jnp.einsum("ns,sfkp->nfkp", placing, sources, preferred_element_type=jnp.float32).astype(
        jnp.bfloat16
    )


def normalize(values, squares, gains):
    scaled = (
        values.astype(jnp.float32)
        * lax.rsqrt(squares / SECTION_CHANNELS + 1e-06)
        * gains.astype(jnp.float32)[:, None]
    )
    return jax.nn.silu(scaled).astype(jnp.bfloat16)


def shards(latents, prior_frame_cache, move_to, counts, norm_gain, conv_weight, conv_bias):
    moved = migrate(prior_frame_cache, move_to)
    slot_count = latents.shape[0]
    frames = latents.shape[1]
    live = (jnp.arange(slot_count) < counts[0])[:, None, None, None]
    start_zero = jnp.zeros(
        (slot_count, frames, conv_weight.shape[1], latents.shape[3]), jnp.float32
    )
    values = latents.astype(jnp.float32)
    partial_squares = jnp.sum(values * values, axis=2, keepdims=True)
    squares = lax.psum(partial_squares, "mp")
    hidden = normalize(latents, squares, norm_gain)
    extended = jnp.concatenate([moved, hidden], axis=1)
    conv_sum = apply_taps(
        start_zero, lax.all_gather(extended, "mp", axis=2, tiled=True), conv_weight, LATENT_COLUMNS
    )
    total = latents.astype(jnp.float32) + conv_sum + conv_bias[:, None]
    decoded = jnp.where(live, total, jnp.zeros_like(total)).astype(jnp.bfloat16)
    new_cache = extended[:, frames:]
    return (decoded, new_cache)


def solution(mesh):
    in_specs = (
        P("req", None, "mp", None),
        P("req", None, "mp", None),
        P("req"),
        P("req"),
        P("mp"),
        P(None, "mp", None),
        P("mp"),
    )
    out_specs = (P("req", None, "mp", None), P("req", None, "mp", None))
    return jax.shard_map(shards, mesh=mesh, in_specs=in_specs, out_specs=out_specs, check_vma=False)
```

profile of v0, /device:TPU:0, one launch (start us, length us, event | category | flops | bytes accessed | tf_op | source)
XLA Modules:
  0.0 157.5 jit_solution(8122907851598073962)
XLA Ops:
  7.2 0.7 fusion.140
  8.3 0.6 select_reduce_fusion.1
  9.5 1.5 collective-permute-start
  11.7 4.0 %collective-permute-start.1 = (bf16[1]{0:T(256)(128)(2,1)}, bf16[1]{0:T(256)(128)(2,1)}, u32[]{:S(2)}, u32[]{:S(2)}) collective-permute-start(bf16[1]{0:T(256)(128)(2,1)} %bitcast.7), channel_id=1, source_target_pairs={{4,0},{8,4},{12,8},{16,12},{20,16},{24,20},{28,24},{0,28},{5,1},{9... | collective-permute-start | bytes 14 | tf_op jit(solution)/shard_map/ppermute | solution.py:13
  15.7 1.4 copy.130
  17.1 0.6 fusion.135
  17.7 0.3 copy.128
  18.1 0.6 fusion.133
  18.7 0.3 copy.129
  19.0 2.7 %collective-permute-start.3 = (bf16[1,2,96,416]{3,0,2,1:T(2,128)(2,1)S(1)}, bf16[1,2,96,416]{3,0,2,1:T(2,128)(2,1)S(1)}, u32[]{:S(2)}, u32[]{:S(2)}) collective-permute-start(bf16[1,2,96,416]{3,0,2,1:T(2,128)(2,1)S(1)} %copy.129), channel_id=1, source_target_pairs={{4,0},{8,4},{12,8},{16,12},{20,16},{24,20},{28,24},{0,28},{5,1},{9... | collective-permute-start | bytes 479240 | tf_op jit(solution)/shard_map/ppermute | solution.py:13
  21.7 12.7 %psum.7 = f32[2,1,1,416]{3,0,2,1:T(2,128)S(1)} all-reduce(f32[2,1,1,416]{3,0,2,1:T(2,128)S(1)} %bitcast.336), channel_id=1, replica_groups=mesh['req'=8,'mp'=4] {'mp'}, use_global_device_ids=true, to_apply=%region_3.4 | all-reduce | flops 832 | bytes 6656 | tf_op jit(solution)/shard_map/psum | solution.py:99
  36.3 1.5 convolution_convert_fusion
  37.8 1.7 %pad_maximum_fusion.2 = bf16[2,3,96,416]{3,0,2,1:T(2,128)(2,1)} fusion(bf16[2,1,96,416]{3,0,2,1:T(2,128)(2,1)S(1)} %copy.131, bf16[2,2,96,416]{3,0,2,1:T(2,128)(2,1)S(1)} %convolution_convert_fusion), kind=kLoop, calls=%fused_computation.110 | loop fusion | flops 239616 | bytes 958464 | tf_op jit(solution)/shard_map/concatenate | solution.py:101
  40.2 0.6 fusion.49
  40.8 0.8 copy.160
  41.6 45.3 %all-gather.2.cloned.1.call-done = bf16[2,3,384,416]{3,0,2,1:T(2,128)(2,1)} async-done(((bf16[2,3,96,416]{3,0,2,1:T(2,128)(2,1)}), bf16[2,3,384,416]{3,0,2,1:T(2,128)(2,1)}) %all-gather.2.cloned.1.call-update) | async-done | bytes 1916944 | tf_op jit(solution)/shard_map/all_gather | solution.py:103
  87.0 18.8 %slice_multiply_fusion.2 = (bf16[2,3,384,624]{3,0,2,1:T(2,128)(2,1)S(1)}, bf16[2,3,384,624]{3,0,2,1:T(2,128)(2,1)S(1)}, bf16[2,3,384,624]{3,0,2,1:T(2,128)(2,1)S(1)}) fusion(bf16[624]{0:T(1024)(128)(2,1)S(1)} %fusion.127, bf16[2,3,384,416]{3,0,2,1:T(2,128)(2,1)} %all-gather.2.cloned.1.call-done, bf16[624]{0:T(1024)(128)(2,1)S(1)} %fusion.129, ...), kind=kLoop, calls=%fused_computation.2 | loop fusion | flops 17252352 | bytes 10546848 | tf_op jit(solution)/shard_map/mul | solution.py:25
  105.8 10.7 %slice_bitcast_fusion.18 = (bf16[2,384,416]{2,0,1:T(2,128)(2,1)S(1)}, bf16[2,384,416]{2,0,1:T(2,128)(2,1)S(1)}, bf16[2,384,416]{2,0,1:T(2,128)(2,1)S(1)}, bf16[2...) fusion(bf16[2,3,384,624]{3,0,2,1:T(2,128)(2,1)S(1)} %get-tuple-, ...), kind=kLoop, calls=%fused_computation.66 | loop fusion | bytes 11501568 | tf_op jit(solution)/shard_map/reshape.33
  116.8 25.4 %slice_bitcast_fusion.8 = (bf16[2,384,416]{2,0,1:T(2,128)(2,1)S(1)}, bf16[2,384,416]{2,0,1:T(2,128)(2,1)S(1)}, bf16[2,384,416]{2,0,1:T(2,128)(2,1)S(1)}, bf16[2,...) fusion(bf16[2,3,384,624]{3,0,2,1:T(2,128)(2,1)S(1)} %get-tuple-, ...), kind=kLoop, calls=%fused_computation.56 | loop fusion | bytes 23003136 | tf_op jit(solution)/shard_map/reshape.53
  145.4 0.3 convolution_add_fusion.13
  145.7 0.3 convolution_add_fusion.12
  145.9 0.3 convolution_add_fusion.11
  146.2 0.3 convolution_add_fusion.10
  146.5 0.3 convolution_add_fusion.9
  146.8 0.3 convolution_add_fusion.8
  147.4 0.3 convolution_add_fusion.6
  147.7 0.3 convolution_add_fusion.5
  148.0 0.3 convolution_add_fusion.4
  148.3 0.3 convolution_add_fusion.3
  148.6 0.3 convolution_add_fusion.2
  148.9 0.3 convolution_add_fusion.1
  149.6 1.1 fusion.17
  (44 shorter events, 5.2 us)
Async XLA Ops:
  7.2 79.8 %all-gather.2.cloned.1.call-start = ((), (), s32[]{:S(2)}) async-start(), calls=%async_computation | async-start | bytes 2949120 | tf_op jit(solution)/shard_map/all_gather | solution.py:103
  9.5 25.4 %collective-permute-start = (bf16[1]{0:T(256)(128)(2,1)}, bf16[1]{0:T(256)(128)(2,1)}, u32[]{:S(2)}, u32[]{:S(2)}) collective-permute-start(bf16[1]{0:T(256)(128)(2,1)} %bitcast.4), channel_id=1, source_target_pairs={{28,0},{0,4},{4,8},{8,12},{12,16},{16,20},{20,24},{24,28},{29,1},{... | collective-permute-start | bytes 14 | tf_op jit(solution)/shard_map/ppermute | solution.py:13
  11.7 23.9 %collective-permute-start.1 = (bf16[1]{0:T(256)(128)(2,1)}, bf16[1]{0:T(256)(128)(2,1)}, u32[]{:S(2)}, u32[]{:S(2)}) collective-permute-start(bf16[1]{0:T(256)(128)(2,1)} %bitcast.7), channel_id=1, source_target_pairs={{4,0},{8,4},{12,8},{16,12},{20,16},{24,20},{28,24},{0,28},{5,1},{9... | collective-permute-start | bytes 14 | tf_op jit(solution)/shard_map/ppermute | solution.py:13
  17.6 4.0 %copy-start.3 = (bf16[96]{0:T(256)(128)(2,1)S(1)}, bf16[96]{0:T(256)(128)(2,1)}, u32[]{:S(2)}) copy-start(bf16[96]{0:T(256)(128)(2,1)} %param.11) | copy-start | bytes 580
  17.6 4.0 %copy-start.1 = (bf16[2,1,96,416]{3,2,1,0:T(8,128)(2,1)S(1)}, bf16[2,1,96,416]{3,2,1,0:T(8,128)(2,1)}, u32[]{:S(2)}) copy-start(bf16[2,1,96,416]{3,2,1,0:T(8,128)(2,1)} %param.7) | copy-start | bytes 479236
  18.0 18.3 %collective-permute-start.2 = (bf16[1,2,96,416]{3,0,2,1:T(2,128)(2,1)S(1)}, bf16[1,2,96,416]{3,0,2,1:T(2,128)(2,1)S(1)}, u32[]{:S(2)}, u32[]{:S(2)}) collective-permute-start(bf16[1,2,96,416]{3,0,2,1:T(2,128)(2,1)S(1)} %copy.128), channel_id=1, source_target_pairs={{28,0},{0,4},{4,8},{8,12},{12,16},{16,20},{20,24},{24,28},{29,1},{... | collective-permute-start | bytes 479240 | tf_op jit(solution)/shard_map/ppermute | solution.py:13
  19.0 17.3 %collective-permute-start.3 = (bf16[1,2,96,416]{3,0,2,1:T(2,128)(2,1)S(1)}, bf16[1,2,96,416]{3,0,2,1:T(2,128)(2,1)S(1)}, u32[]{:S(2)}, u32[]{:S(2)}) collective-permute-start(bf16[1,2,96,416]{3,0,2,1:T(2,128)(2,1)S(1)} %copy.129), channel_id=1, source_target_pairs={{4,0},{8,4},{12,8},{16,12},{20,16},{24,20},{28,24},{0,28},{5,1},{9... | collective-permute-start | bytes 479240 | tf_op jit(solution)/shard_map/ppermute | solution.py:13
  105.8 10.7 %copy-start = (bf16[27,96,384]{2,1,0:T(8,128)(2,1)S(1)}, bf16[27,96,384]{2,1,0:T(8,128)(2,1)}, u32[]{:S(2)}) copy-start(bf16[27,96,384]{2,1,0:T(8,128)(2,1)} %param.12) | copy-start | bytes 5971972
  148.9 0.7 copy-start.2
Sparse Core Ops, SparseCore 0:
  39.7 47.2 all-gather.1
where the time goes:
time: 158 us
  waiting for transfers between devices  45.3 us (29%)
  local copies, waits for them, and re-layouts  39.2 us (25%)
  other arithmetic  23.1 us (15%)
  between operations  17.7 us (11%)
  blocking collectives  12.7 us (8%)
  matrix products  11.2 us (7%)
  starting transfers between devices  8.27 us (5%)
    all_gather x1, waiting for transfers between devices, shards(): lax.all_gather(extended, 'mp', axis=2, tiled=True)  45.3 us
    another operation x2, local copies, waits for them, and re-layouts  36.1 us
    mul x1, other arithmetic, apply_taps(): shifted = padded[:, :, :, step_x:step_x + pixels + 2 * row_width] * inside  18.8 us
    psum x1, blocking collectives, shards(): squares = lax.psum(partial_squares, 'mp')  12.7 us
    dot_general x27, matrix products, apply_taps(): jnp.einsum('oc,stcp->stop', weights[step_t * 9 + step_y * 3 + step_x], wi...  8.54 us
    ppermute x4, starting transfers between devices, shifted_2(): return lax.ppermute(block, axis, route)  8.23 us
  transfers between devices with their start and end apart: 5, of which 1 were waited for; matrix products, arithmetic and copies ran while one was open for 3% of the time, Pallas kernels for 0%

commit v1 on v0

--- a/solution.py
+++ b/solution.py
@@ -5,6 +5,28 @@
 
 SECTION_CHANNELS = 384
 LATENT_COLUMNS = 104
+
+
+def in_order(parts, dim):
+    parts = jnp.moveaxis(parts, 0, dim)
+    shape = parts.shape
+    return parts.reshape(*shape[:dim], shape[dim] * shape[dim + 1], *shape[dim + 2 :])
+
+
+def collected_by_bits(shard, axis):
+    size = lax.axis_size(axis)
+    blocks = shard[None]
+    for level in range(size.bit_length() - 1):
+        apart = 1 << level
+        received = lax.ppermute(blocks, axis, [(i, i ^ apart) for i in range(size)])
+        both = jnp.stack([blocks, received])
+        upper = lax.axis_index(axis) >> level & 1
+        blocks = jnp.where(upper == 0, both, both[::-1]).reshape(-1, *shard.shape)
+    return blocks
+
+
+def gather_by_bits(x, axis, dim):
+    return in_order(collected_by_bits(x, axis), dim)
 
 
 def shifted_2(block, axis, distance):
@@ -100,7 +122,7 @@
     hidden = normalize(latents, squares, norm_gain)
     extended = jnp.concatenate([moved, hidden], axis=1)
     conv_sum = apply_taps(
-        start_zero, lax.all_gather(extended, "mp", axis=2, tiled=True), conv_weight, LATENT_COLUMNS
+        start_zero, gather_by_bits(extended, "mp", 2), conv_weight, LATENT_COLUMNS
     )
     total = latents.astype(jnp.float32) + conv_sum + conv_bias[:, None]
     decoded = jnp.where(live, total, jnp.zeros_like(total)).astype(jnp.bfloat16)

time: 158 us -> 126 us (0.80); the launches traced: 158 us -> 124 us
  local copies, waits for them, and re-layouts: 39.2 us -> 5.95 us
  between operations: 17.7 us -> 4.16 us
  waiting for transfers between devices: 45.3 us -> 57.7 us
  other arithmetic: 23.1 us -> 21 us
  matrix products: 11.2 us -> 12.8 us
    ppermute x0 -> x2, waiting for transfers between devices: none -> 57.7 us  [collected_by_bits(): received = lax.ppermute(blocks, axis, [(i, i ^ apart) for i in range(size)])]
    all_gather x1 -> x0, waiting for transfers between devices: 45.3 us -> none  [shards(): lax.all_gather(extended, 'mp', axis=2, tiled=True)]
    another operation x2 -> x0, local copies, waits for them, and re-layouts: 36.1 us -> none
    mul x1, other arithmetic: 18.8 us -> 5.69 us  [apply_taps(): shifted = padded[:, :, :, step_x:step_x + pixels + 2 * row_width] * inside]
    another operation x3 -> x7, other arithmetic: 0.35 us -> 10.5 us  [the longest x4 10.1 us: collected_by_bits(): both = jnp.stack([blocks, received])]
    reshape x0 -> x2, local copies, waits for them, and re-layouts: none -> 2.86 us  [the longest x1 2.37 us: in_order(): parts.reshape(*shape[:dim], shape[dim] * shape[dim + 1], *shape[dim + 2:])]
    select_n x0 -> x1, other arithmetic: none -> 2.54 us  [collected_by_bits(): blocks = jnp.where(upper == 0, both, both[::-1]).reshape(-1, *shard.shape)]
    concatenate x2 -> x1, other arithmetic: 2.28 us -> 0.59 us  [shards(): extended = jnp.concatenate([moved, hidden], axis=1)]
  transfers between devices with their start and end apart: 5 -> 6, of which waited for: 1 -> 2; matrix products, arithmetic and copies ran while one was open for 3% -> 4% of each run, Pallas kernels for 0% -> 0%
where the time goes in v1:
time: 126 us; the launch traced here: 124 us
  waiting for transfers between devices  57.7 us (46%)
  other arithmetic  21 us (17%)
  matrix products  12.8 us (10%)
  blocking collectives  12.7 us (10%)
  starting transfers between devices  9.49 us (8%)
  local copies, waits for them, and re-layouts  5.95 us (5%)
  between operations  4.16 us (3%)
    ppermute x2, waiting for transfers between devices, collected_by_bits(): received = lax.ppermute(blocks, axis, [(i, i ^ apart) for i in range(size)])  57.7 us
    psum x1, blocking collectives, shards(): squares = lax.psum(partial_squares, 'mp')  12.7 us
    dot_general x27, matrix products, apply_taps(): jnp.einsum('oc,stcp->stop', weights[step_t * 9 + step_y * 3 + step_x], wi...  10.2 us
    another operation x4, other arithmetic, collected_by_bits(): both = jnp.stack([blocks, received])  10.1 us
    ppermute x4, starting transfers between devices, shifted_2(): return lax.ppermute(block, axis, route)  8.23 us
    mul x1, other arithmetic, apply_taps(): shifted = padded[:, :, :, step_x:step_x + pixels + 2 * row_width] * inside  5.69 us
    select_n x1, other arithmetic, collected_by_bits(): blocks = jnp.where(upper == 0, both, both[::-1]).reshape(-1, *shard.shape)  2.54 us
  transfers between devices with their start and end apart: 6, of which 2 were waited for; matrix products, arithmetic and copies ran while one was open for 4% of the time, Pallas kernels for 0%

profile of v1, /device:TPU:0, one launch (start us, length us, event | category | flops | bytes accessed | tf_op | source)
XLA Modules:
  0.0 123.9 jit_solution(8398442726041553217)
XLA Ops:
  0.6 0.7 fusion.118
  1.7 0.6 select_reduce_fusion.1
  2.9 1.5 %collective-permute-start = (bf16[1]{0:T(256)(128)(2,1)}, bf16[1]{0:T(256)(128)(2,1)}, u32[]{:S(2)}, u32[]{:S(2)}) collective-permute-start(bf16[1]{0:T(256)(128)(2,1)} %bitcast.4), channel_id=1, source_target_pairs={{28,0},{0,4},{4,8},{8,12},{12,16},{16,20},{20,24},{24,28},{29,1},{... | collective-permute-start | bytes 14 | tf_op jit(solution)/shard_map/ppermute | solution.py:35
  5.1 4.0 %collective-permute-start.1 = (bf16[1]{0:T(256)(128)(2,1)}, bf16[1]{0:T(256)(128)(2,1)}, u32[]{:S(2)}, u32[]{:S(2)}) collective-permute-start(bf16[1]{0:T(256)(128)(2,1)} %bitcast.7), channel_id=1, source_target_pairs={{4,0},{8,4},{12,8},{16,12},{20,16},{24,20},{28,24},{0,28},{5,1},{9... | collective-permute-start | bytes 14 | tf_op jit(solution)/shard_map/ppermute | solution.py:35
  9.1 1.4 %copy.79 = bf16[2,2,96,416]{3,0,2,1:T(2,128)(2,1)S(1)} copy(bf16[2,2,96,416]{3,2,1,0:T(8,128)(2,1)} %param.8) | data formatting | bytes 638976 | tf_op args[1]
  10.5 0.6 fusion.113
  11.5 0.6 fusion.111
  12.4 2.7 %collective-permute-start.3 = (bf16[1,2,96,416]{3,0,2,1:T(2,128)(2,1)S(1)}, bf16[1,2,96,416]{3,0,2,1:T(2,128)(2,1)S(1)}, u32[]{:S(2)}, u32[]{:S(2)}) collective-permute-start(bf16[1,2,96,416]{3,0,2,1:T(2,128)(2,1)S(1)} %copy.78), channel_id=1, source_target_pairs={{4,0},{8,4},{12,8},{16,12},{20,16},{24,20},{28,24},{0,28},{5,1},{9... | collective-permute-start | bytes 479240 | tf_op jit(solution)/shard_map/ppermute | solution.py:35
  15.2 12.7 %psum.7 = f32[2,1,1,416]{3,0,2,1:T(2,128)S(1)} all-reduce(f32[2,1,1,416]{3,0,2,1:T(2,128)S(1)} %bitcast.380), channel_id=1, replica_groups=mesh['req'=8,'mp'=4] {'mp'}, use_global_device_ids=true, to_apply=%region_3.4 | all-reduce | flops 832 | bytes 6656 | tf_op jit(solution)/shard_map/psum | solution.py:121
  29.7 1.5 %convolution_convert_fusion = bf16[2,2,96,416]{3,0,2,1:T(2,128)(2,1)S(1)} fusion(bf16[1,2,96,416]{3,0,2,1:T(2,128)(2,1)S(1)} %collective-permute-done.3, bf16[1,2,96,416]{3,0,2,1:T(2,128)(2,1)S(1)} %collective-permute-done.2, bf16[2,2,96,416]{3,0,2,1:T(2,128)(2,1)S(1)} %copy.79, f32[4]{0:T(128)S(1)} %pad_maximum_fusion.5), kind=kOutput, calls=%fused_computation.9 | convolution fusion | flops 3354632 | bytes 958480 | tf_op jit(solution)/shard_map/ns,sfkp->nfkp/dot_general | solution.py:97
  31.2 1.0 fusion.123
  32.3 11.3 %collective-permute-done.4 = bf16[1,2,3,96,416]{4,1,3,2,0:T(2,128)(2,1)S(1)} collective-permute-done((bf16[1,2,3,96,416]{4,1,3,2,0:T(2,128)(2,1)S(1)}, bf16[1,2,3,96,416]{4,1,3,2,0:T(2,128)(2,1)S(1)}, u32[]{:S(2)}, u32[]{:S(2)}) %collective-permute-start.4) | collective-permute-done | bytes 479264 | tf_op jit(solution)/shard_map/ppermute | solution.py:21
  43.6 1.8 %pad_maximum_fusion.1 = bf16[2,1,2,3,96,416]{5,2,4,3,1,0:T(2,128)(2,1)S(1)} fusion(bf16[1,1,2,3,96,416]{5,2,4,3,1,0:T(2,128)(2,1)S(1)} %bitcast.379, bf16[1,1,2,3,96,416]{5,2,4,3,1,0:T(2,128)(2,1)S(1)} %get-tuple-element.18), kind=kLoop, calls=%fused_computation.52 | loop fusion | flops 479232 | bytes 1916928 | tf_op jit(solution)/shard_map/stack | solution.py:22
  45.4 2.6 %fusion.91 = (bf16[1,2,2,3,96,416]{5,2,4,3,1,0:T(2,128)(2,1)S(1)}, bf16[2,2,3,96,416]{4,1,3,2,0:T(2,128)(2,1)}) fusion(bf16[2,1,2,3,96,416]{5,2,4,3,1,0:T(2,128)(2,1)S(1)} %pad_maximum_fusion.1, pred[]{:T(512)S(6)} %eq.48), kind=kLoop, calls=%fused_computation.160 | loop fusion | flops 479232 | bytes 2875393 | tf_op jit(solution)/shard_map/stack;reshape | solution.py:22
  48.0 1.2 collective-permute-start.5
  49.9 0.6 fusion.25
  50.5 0.8 copy.84
  51.3 46.4 %collective-permute-done.5 = bf16[2,2,3,96,416]{4,1,3,2,0:T(2,128)(2,1)} collective-permute-done((bf16[2,2,3,96,416]{4,1,3,2,0:T(2,128)(2,1)}, bf16[2,2,3,96,416]{4,1,3,2,0:T(2,128)(2,1)}, u32[]{:S(2)}, u32[]{:S(2)}) %collective-permute-start.5) | collective-permute-done | bytes 958496 | tf_op jit(solution)/shard_map/ppermute | solution.py:21
  97.7 4.8 %pad_maximum_fusion = bf16[2,2,2,3,96,416]{5,2,4,3,1,0:T(2,128)(2,1)S(1)} fusion(bf16[1,2,2,3,96,416]{5,2,4,3,1,0:T(2,128)(2,1)} %bitcast.25, bf16[1,2,2,3,96,416]{5,2,4,3,1,0:T(2,128)(2,1)S(1)} %get-tuple-element.16), kind=kLoop, calls=%fused_computation.7 | loop fusion | flops 958464 | bytes 3833856 | tf_op jit(solution)/shard_map/stack | solution.py:22
  102.5 2.5 %broadcast_select_fusion = bf16[2,2,2,3,96,416]{5,2,4,3,1,0:T(2,128)(2,1)S(1)} fusion(bf16[2,2,2,3,96,416]{5,2,4,3,1,0:T(2,128)(2,1)S(1)} %pad_maximum_fusion, pred[]{:T(512)S(6)} %eq.47), kind=kLoop, calls=%fused_computation | loop fusion | flops 958464 | bytes 3833857 | tf_op jit(solution)/shard_map/jit(_where)/select_n | solution.py:24
  105.0 0.5 copy.81
  105.5 2.4 %copy.82 = bf16[2,3,384,416]{2,3,0,1:T(8,128)(2,1)} copy(bf16[2,3,384,416]{3,2,1,0:T(8,128)(2,1)S(1)} %bitcast.378) | data formatting | bytes 3833856 | tf_op jit(solution)/shard_map/reshape | solution.py:13
  107.9 5.7 %fusion = (bf16[2,3,384,624]{2,3,0,1:T(8,128)(2,1)S(1)}, bf16[2,3,384,624]{2,3,0,1:T(8,128)(2,1)S(1)}, bf16[2,3,384,624]{2,3,0,1:T(8,128)(2,1)S(1)}) fusion(bf16[2,3,384,416]{2,3,0,1:T(8,128)(2,1)} %copy.82, bf16[624]{0:T(1024)(128)(2,1)S(1)} %get-tuple-element.23, bf16[624]{0:T(1024)(128)(2,1)S(1)} %fusion.107, bf16[624]{0:T(1024)(128)(2,1)S(1)} %get-tuple-element.22), kind=kLoop, calls=%fused_computation.4 | loop fusion | flops 17252352 | bytes 10546848 | tf_op jit(solution)/shard_map/mul | solution.py:47
  114.0 0.3 convolution_bitcast_fusion.1
  114.3 0.3 convolution_bitcast_fusion.2
  116.1 0.3 convolution_bitcast_fusion.7
  120.2 0.3 convolution_add_fusion.6
  120.6 0.4 convolution_add_fusion.5
  120.9 0.4 convolution_add_fusion.4
  121.3 0.3 convolution_add_fusion.3
  122.3 0.3 fusion.3
  122.7 1.2 fusion.20
  (48 shorter events, 8.0 us)
Async XLA Ops:
  2.9 25.4 %collective-permute-start = (bf16[1]{0:T(256)(128)(2,1)}, bf16[1]{0:T(256)(128)(2,1)}, u32[]{:S(2)}, u32[]{:S(2)}) collective-permute-start(bf16[1]{0:T(256)(128)(2,1)} %bitcast.4), channel_id=1, source_target_pairs={{28,0},{0,4},{4,8},{8,12},{12,16},{16,20},{20,24},{24,28},{29,1},{... | collective-permute-start | bytes 14 | tf_op jit(solution)/shard_map/ppermute | solution.py:35
  5.1 23.9 %collective-permute-start.1 = (bf16[1]{0:T(256)(128)(2,1)}, bf16[1]{0:T(256)(128)(2,1)}, u32[]{:S(2)}, u32[]{:S(2)}) collective-permute-start(bf16[1]{0:T(256)(128)(2,1)} %bitcast.7), channel_id=1, source_target_pairs={{4,0},{8,4},{12,8},{16,12},{20,16},{24,20},{28,24},{0,28},{5,1},{9... | collective-permute-start | bytes 14 | tf_op jit(solution)/shard_map/ppermute | solution.py:35
  10.5 4.6 %copy-start.3 = (bf16[96]{0:T(256)(128)(2,1)S(1)}, bf16[96]{0:T(256)(128)(2,1)}, u32[]{:S(2)}) copy-start(bf16[96]{0:T(256)(128)(2,1)} %param.11) | copy-start | bytes 580
  10.5 4.6 %copy-start.1 = (bf16[2,1,96,416]{3,2,1,0:T(8,128)(2,1)S(1)}, bf16[2,1,96,416]{3,2,1,0:T(8,128)(2,1)}, u32[]{:S(2)}) copy-start(bf16[2,1,96,416]{3,2,1,0:T(8,128)(2,1)} %param.7) | copy-start | bytes 479236
  11.4 18.3 %collective-permute-start.2 = (bf16[1,2,96,416]{3,0,2,1:T(2,128)(2,1)S(1)}, bf16[1,2,96,416]{3,0,2,1:T(2,128)(2,1)S(1)}, u32[]{:S(2)}, u32[]{:S(2)}) collective-permute-start(bf16[1,2,96,416]{3,0,2,1:T(2,128)(2,1)S(1)} %copy.77), channel_id=1, source_target_pairs={{28,0},{0,4},{4,8},{8,12},{12,16},{16,20},{20,24},{24,28},{29,1},{... | collective-permute-start | bytes 479240 | tf_op jit(solution)/shard_map/ppermute | solution.py:35
  12.4 17.3 %collective-permute-start.3 = (bf16[1,2,96,416]{3,0,2,1:T(2,128)(2,1)S(1)}, bf16[1,2,96,416]{3,0,2,1:T(2,128)(2,1)S(1)}, u32[]{:S(2)}, u32[]{:S(2)}) collective-permute-start(bf16[1,2,96,416]{3,0,2,1:T(2,128)(2,1)S(1)} %copy.78), channel_id=1, source_target_pairs={{4,0},{8,4},{12,8},{16,12},{20,16},{24,20},{28,24},{0,28},{5,1},{9... | collective-permute-start | bytes 479240 | tf_op jit(solution)/shard_map/ppermute | solution.py:35
  32.2 11.4 %collective-permute-start.4 = (bf16[1,2,3,96,416]{4,1,3,2,0:T(2,128)(2,1)S(1)}, bf16[1,2,3,96,416]{4,1,3,2,0:T(2,128)(2,1)S(1)}, u32[]{:S(2)}, u32[]{:S(2)}) collective-permute-start(bf16[1,2,3,96,416]{4,1,3,2,0:T(2,128)(2,1)S(1)} %get-tuple-element.19), channel_id=1, source_target_pairs={{0,1},{1,0},{2,3},{3,2},{4,5},{5,4},{6,7},{7,6},{8,9},{9,8},{10,11... | collective-permute-start | bytes 1437704 | tf_op jit(solution)/shard_map/ppermute | solution.py:21
  48.0 49.7 %collective-permute-start.5 = (bf16[2,2,3,96,416]{4,1,3,2,0:T(2,128)(2,1)}, bf16[2,2,3,96,416]{4,1,3,2,0:T(2,128)(2,1)}, u32[]{:S(2)}, u32[]{:S(2)}) collective-permute-start(bf16[2,2,3,96,416]{4,1,3,2,0:T(2,128)(2,1)} %get-tuple-element.17), channel_id=1, source_target_pairs={{0,2},{1,3},{2,0},{3,1},{4,6},{5,7},{6,4},{7,5},{8,10},{9,11},{10,... | collective-permute-start | bytes 2875400 | tf_op jit(solution)/shard_map/ppermute | solution.py:21
  107.9 5.7 %copy-start = (bf16[27,96,384]{2,1,0:T(8,128)(2,1)S(1)}, bf16[27,96,384]{2,1,0:T(8,128)(2,1)}, u32[]{:S(2)}) copy-start(bf16[27,96,384]{2,1,0:T(8,128)(2,1)} %param.12) | copy-start | bytes 5971972
  121.6 1.1 copy-start.2
